TPU v7x, 256 devices: a whole 4x4x8 slice. The times are simulated.
256 devices in a mesh: dom: 32 (over z, x), head: 8 (over y, core).
Axes of the slice: x: 4, y: 4, z: 8, core: 2. Of those that a mesh axis runs over, the one named last changes fastest.
Arguments:
- node_feats: float32 [32768, 512], P('dom')
- order: int32 [32768], P('dom'), may hold values from 0 to 32767, as said below
- node_count: int32 [256], replicated, may hold values from 32 to 128
- local_blocks: int32 [256, 3], P('dom'), may hold values from 0 to 255, as said below
- exp_blocks: int32 [256, 6], P('dom'), may hold values from 0 to 255, as said below
- virt_blocks: int32 [256], P('dom'), may hold values from 0 to 3
- virt_feats: float32 [512, 512], replicated, may hold values from -6 to 6
- w_query: float32 [512, 512], P(None, 'head'), may hold values from -0.25 to 0.25
- w_key: float32 [512, 512], P(None, 'head'), may hold values from -0.25 to 0.25
- w_value: float32 [512, 512], P(None, 'head'), may hold values from -0.25 to 0.25
- w_out: float32 [512, 512], P(None, 'head'), may hold values from -2 to 2
- w_up: float32 [512, 1024], P(None, 'head'), may hold values from -0.25 to 0.25
- w_down: float32 [1024, 512], P('head'), may hold values from -0.1875 to 0.1875
Outputs:
- refined: float32 [32768, 512], P('dom', 'head')
Inputs may be any that keep to these rules, and one draw needn't show every extreme that they name: `order`: each device's 8 * 128 entries are a permutation of that device's own node numbers (the rows it holds). `local_blocks`: every entry lies within 2 clusters of its own cluster; column 1 is exactly 2 away unless that leaves the grid, where it is clipped to the end. `exp_blocks`: call id // 8 the owner of a cluster id. Among the 48 entries of one device's clusters, at most 3 have any one owner, and for every device some owner has exactly 3.
All inputs are finite; a program needn't handle non-finite values.
Results may differ from a plain program's by a relative error of at most 0.0003.
Values sent between devices are 32-bit elements; how exact they have to be, the bound alone decides.
No kernel may reach another device: no remote copies, remote signals or barrier semaphores. Data moves between devices by JAX's collectives and lax.ppermute only.
A program may use at most 128 MiB of HBM per device.

v0:
```python
import math
import jax
import jax.numpy as jnp
from jax import lax
from jax.sharding import PartitionSpec as P

D = 512
HD = 64
NE = 6
LW = 2
highest = lax.Precision.HIGHEST


def with_halo(value, sides, width):
    for axis, dim in sides:
        size, length = (lax.axis_size(axis), value.shape[dim])
        up = [(i, (i + 1) % size) for i in range(size - 1)]
        down = [(j, i) for i, j in up]
        last = lax.slice_in_dim(value, length - width, length, axis=dim)
        initial = lax.slice_in_dim(value, 0, width, axis=dim)
        before = lax.ppermute(last, axis, up)
        after = lax.ppermute(initial, axis, down)
        value = jnp.concatenate([before, value, after], axis=dim)
    return value


def matmul(left, right):
    return jnp.dot(left, right, preferred_element_type=jnp.float32, precision=highest)


def partial_softmax(queries, keyvals, usable, head_width):
    batch_size = queries.shape[0]
    head_count = queries.shape[2]
    head_size = queries.shape[3]
    key_rows = keyvals[..., :head_width].reshape(batch_size, -1, head_count, head_size)
    value_rows = keyvals[..., head_width:].reshape(batch_size, -1, head_count, head_size)
    scores = jnp.einsum("bqhd,bkhd->bhqk", queries, key_rows, precision=highest) / math.sqrt(
        head_size
    )
    scores = jnp.where(usable[:, None, None, :], scores, -1e30)
    peaks = jnp.max(scores, axis=3)
    weights = jnp.where(usable[:, None, None, :], jnp.exp(scores - peaks[..., None]), 0.0)
    totals = jnp.sum(weights, axis=3)
    weighted = jnp.einsum("bhqk,bkhd->bqhd", weights, value_rows, precision=highest)
    return (peaks, totals, weighted)


def shards(
    node_feats,
    order,
    node_count,
    local_blocks,
    exp_blocks,
    virt_blocks,
    virt_feats,
    w_query,
    w_key,
    w_value,
    w_out,
    w_up,
    w_down,
):
    dom_size = lax.axis_size("dom")
    clus_dev = local_blocks.shape[0]
    rows_dev = node_feats.shape[0]
    clus_rows = rows_dev // clus_dev
    head_width = w_query.shape[1]
    head_count = head_width // HD
    capacity = max(2, 5 * clus_dev * NE // (2 * dom_size))
    base_row = lax.axis_index("dom") * rows_dev
    first_cluster = lax.axis_index("dom") * clus_dev
    local_order = order - base_row
    ordered = jnp.take(node_feats, local_order, axis=0)
    queries = matmul(ordered, w_query).reshape(clus_dev, clus_rows, head_count, HD)
    keyvals = jnp.concatenate([matmul(ordered, w_key), matmul(ordered, w_value)], 1).reshape(
        clus_dev, clus_rows, 2 * head_width
    )
    virt_kv = jnp.concatenate([matmul(virt_feats, w_key), matmul(virt_feats, w_value)], 1).reshape(
        -1, clus_rows, 2 * head_width
    )
    virt_near = jnp.take(virt_kv, virt_blocks, axis=0)
    positions = jnp.arange(clus_rows)

    def row_usable(block_ids):
        return positions < jnp.take(node_count, block_ids)[..., None]

    padded = with_halo(keyvals, (("dom", 0),), LW)
    near_kv = jnp.take(padded, local_blocks - (first_cluster - LW), axis=0)
    near_usable = row_usable(local_blocks)
    virt_usable = jnp.ones((clus_dev, 1, clus_rows), bool)
    far_usable = row_usable(exp_blocks)
    flat_ids = exp_blocks.reshape(-1)
    owners = flat_ids // clus_dev
    inside = flat_ids % clus_dev
    onehot = (owners[:, None] == jnp.arange(dom_size)[None, :]).astype(jnp.int32)
    slots = jnp.sum((jnp.cumsum(onehot, 0) - onehot) * onehot, 1)
    request = jnp.zeros((dom_size, capacity), jnp.int32).at[owners, slots].set(inside)
    blocks = jnp.take(
        keyvals, lax.all_to_all(request, "dom", split_axis=0, concat_axis=0, tiled=True), axis=0
    )
    arrived = lax.all_to_all(blocks, "dom", split_axis=0, concat_axis=0, tiled=True)
    far_kv = arrived[owners, slots].reshape(clus_dev, NE, clus_rows, 2 * head_width)
    every_kv = jnp.concatenate([near_kv, far_kv, virt_near[:, None]], 1).reshape(
        clus_dev, -1, 2 * head_width
    )
    every_usable = jnp.concatenate([near_usable, far_usable, virt_usable], 1).reshape(clus_dev, -1)
    peaks, totals, weighted = partial_softmax(queries, every_kv, every_usable, head_width)
    attention = weighted / jnp.transpose(totals, (0, 2, 1))[..., None]
    heads_flat = attention.reshape(rows_dev, head_width)
    col_width = w_out.shape[1]
    projected = matmul(lax.all_gather(heads_flat, "head", axis=1, tiled=True), w_out)
    col_start = lax.axis_index("head") * col_width
    residual = lax.dynamic_slice_in_dim(ordered, col_start, col_width, 1) + projected
    row_sums, row_squares = lax.psum(
        (jnp.sum(residual, 1), jnp.sum(residual * residual, 1)), "head"
    )
    row_mean = row_sums / D
    row_var = row_squares / D - row_mean * row_mean
    normed = (residual - row_mean[:, None]) * lax.rsqrt(row_var + 1e-05)[:, None]
    hidden = matmul(lax.all_gather(normed, "head", axis=1, tiled=True), w_up)
    activated = jax.nn.gelu(hidden, approximate=False)
    partials = matmul(activated, w_down)
    feed_forward = lax.psum_scatter(partials, "head", scatter_dimension=1, tiled=True)
    result = residual + feed_forward
    return jnp.zeros_like(result).at[local_order].set(result)


def solution(mesh):
    return jax.shard_map(
        shards,
        mesh=mesh,
        in_specs=(
            P("dom", None),
            P("dom"),
            P(),
            P("dom", None),
            P("dom", None),
            P("dom"),
            P(),
            P(None, "head"),
            P(None, "head"),
            P(None, "head"),
            P(None, "head"),
            P(None, "head"),
            P("head", None),
        ),
        out_specs=P("dom", "head"),
        check_vma=False,
    )
```

profile of v0, /device:TPU:2, one launch (start us, length us, event | category | flops | bytes accessed | tf_op | source)
XLA Modules:
  0.0 362.6 jit_solution(8832196854405304521)
XLA Ops:
  6.5 0.9 reshape.232
  7.5 0.8 reshape.231
  8.4 0.2 select_reduce_fusion
  8.6 2.8 scatter_fusion
  11.4 0.7 copy.52
  12.1 11.6 %all-to-all-start = ((s32[32,1,3]{2,1,0:T(1,128)}), s32[32,1,3]{2,1,0:T(1,128)S(1)}, u32[]{:S(2)}, u32[]{:S(2)}) async-start(s32[32,1,3]{2,1,0:T(1,128)} %copy.52), calls=%async_computation | async-start | bytes 32768 | tf_op jit(solution)/shard_map/all_to_all | solution.py:99
  23.7 0.7 compare_and_fusion.1
  24.4 4.9 %gather_fusion = f32[1024,512]{1,0:T(8,128)} fusion(f32[1024,512]{1,0:T(8,128)S(1)} %copy-done, s32[1024]{0:T(1024)S(1)} %broadcast_clamp_fusion), kind=kCustom, calls=%fused_computation | custom fusion | bytes 4198400 | tf_op jit(solution)/shard_map/jit(_take)/gather | solution.py:73
  29.3 2.9 copy.47
  32.2 1.8 broadcast_select_fusion.1
  34.0 1.5 fusion.153
  35.5 1.5 fusion.152
  37.0 0.8 pad_maximum_fusion.2
  37.8 1.2 copy.74
  39.1 0.1 copy.56
  39.2 0.1 reshape.256
  39.4 0.1 copy.54
  39.6 3.6 gather_fusion.2
  43.2 5.9 %broadcast_select_fusion = f32[32,3,128,128]{3,2,1,0:T(8,128)} fusion(f32[32,3,128,128]{3,2,1,0:T(8,128)} %bitcast.82, pred[32,3]{1,0:T(8,128)(4,1)S(1)} %copy.54), kind=kLoop, calls=%fused_computation.17 | loop fusion | flops 1572864 | bytes 12583008 | tf_op jit(solution)/shard_map/jit(_take)/select_n | solution.py:98
  49.1 9.8 %all-to-all-start.1 = ((f32[32,3,128,128]{3,2,1,0:T(8,128)}), f32[32,3,128,128]{3,2,1,0:T(8,128)}, u32[]{:S(2)}, u32[]{:S(2)}) async-start(f32[32,3,128,128]{3,2,1,0:T(8,128)} %broadcast_select_fusion), calls=%async_computation.1 | async-start | bytes 12582912 | tf_op jit(solution)/shard_map/all_to_all | solution.py:101
  59.0 0.7 fusion.113
  59.7 1.7 copy.72
  61.3 2.2 collective-permute-start.1
  63.5 0.8 copy.71
  64.3 4.1 %collective-permute-start = (f32[2,128,128]{2,1,0:T(8,128)}, f32[2,128,128]{2,1,0:T(8,128)}, u32[]{:S(2)}, u32[]{:S(2)}) collective-permute-start(f32[2,128,128]{2,1,0:T(8,128)} %bitcast), channel_id=1, source_target_pairs={{0,8},{8,16},{16,24},{24,32},{32,40},{40,48},{48,56},{56,64},{64,7... | collective-permute-start | bytes 393224 | tf_op jit(solution)/shard_map/ppermute | solution.py:21
  68.4 2.4 fusion.155
  70.7 2.4 fusion.154
  73.1 0.1 copy.73
  73.3 0.8 copy.48
  74.0 0.1 reshape.286
  74.1 0.8 gather_fusion.6
  75.0 0.1 copy.65
  75.1 0.1 reshape.278
  75.2 0.7 gather_fusion.5
  75.9 0.1 reshape.277
  76.0 0.1 copy.64
  76.1 0.6 gather_fusion.4
  76.9 0.9 fusion.23
  77.9 3.7 %convolution_bitcast_fusion = f32[8,8,8,128]{3,2,1,0:T(8,128)} fusion(f32[1024,512]{0,1:T(8,128)} %copy-done.2, f32[512,64]{0,1:T(8,128)} %param.20), kind=kOutput, calls=%fused_computation.22 | convolution fusion | flops 402653184 | bytes 2490368 | tf_op jit(solution)/shard_map/dot_general | solution.py:28
  81.7 3.4 collective-permute-done.1
  85.2 1.0 pad_maximum_fusion.1
  86.2 1.8 gather_fusion.1
  88.0 2.8 broadcast_select_fusion.2
  90.7 106.3 %all-to-all-done.1 = f32[32,3,128,128]{3,2,1,0:T(8,128)} async-done(((f32[32,3,128,128]{3,2,1,0:T(8,128)}), f32[32,3,128,128]{3,2,1,0:T(8,128)}, u32[]{:S(2)}, u32[]{:S(2)}) %all-to-all-start.1) | async-done | bytes 6291488 | tf_op jit(solution)/shard_map/all_to_all | solution.py:101
  197.0 5.4 %gather_fusion.3 = f32[48,128,128]{2,1,0:T(8,128)} fusion(f32[32,3,128,128]{3,2,1,0:T(8,128)} %all-to-all-done.1, s32[48]{0:T(128)S(1)} %get-tuple-element.11), kind=kCustom, calls=%fused_computation.3 | custom fusion | bytes 6291840 | tf_op jit(solution)/shard_map/gather | solution.py:102
  202.5 2.8 pad_maximum_fusion
  205.3 6.1 %fusion.151 = (f32[8,128]{1,0:T(8,128)S(1)}, f32[8,128,1280]{2,1,0:T(8,128)S(1)}) fusion(f32[8,1280,128]{2,1,0:T(8,128)S(1)} %bitcast.80, f32[8,8,8,128]{3,2,1,0:T(8,128)S(1)} %copy-done.4, pred[8,1280]{1,0:T(8,128)(4,1)S(1)} %add_bitcast_fusion), kind=kOutput, calls=%fused_computation.216 | convolution fusion | flops 1010564096 | bytes 10762240 | tf_op jit(solution)/shard_map/bqhd,bkhd->bhqk/dot_general | solution.py:37
  211.3 1.1 fusion.6
  212.5 10.5 %fusion.16 = f32[8,128,1,64]{1,3,0,2:T(8,128)S(1)} fusion(f32[8,128,1280]{2,1,0:T(8,128)S(1)} %get-tuple-element.22, f32[8,128]{1,0:T(8,128)S(1)} %get-tuple-element.21, pred[8,1280]{1,0:T(8,128)(4,1)S(1)} %add_bitcast_fusion, f32[8,1280,128]{2,1,0:T(8,128)S(1)} %bitcast.81, f32[8,128]{1,0:T(8,128)S(1)} %fusion.6), kind=kOutput, calls=%fused_computation.25 | convolution fusion | flops 1009319936 | bytes 10766336 | tf_op jit(solution)/shard_map/bhqk,bkhd->bqhd/dot_general | solution.py:44
  223.0 0.2 copy.68
  223.2 0.8 copy.86
  224.0 35.8 %all-gather.3.cloned.1.call-done = f32[1024,512]{0,1:T(8,128)} async-done(((f32[1024,64]{0,1:T(8,128)}), f32[1024,512]{0,1:T(8,128)}) %all-gather.3.cloned.1.call-update) | async-done | bytes 2097168 | tf_op jit(solution)/shard_map/all_gather | solution.py:111
  259.8 3.0 fusion.150
  262.9 14.2 %all-reduce = (f32[1024]{0:T(1024)S(1)}, f32[1024]{0:T(1024)S(1)}) all-reduce(f32[1024]{0:T(1024)S(1)} %get-tuple-element.6, f32[1024]{0:T(1024)S(1)} %get-tuple-element.5), channel_id=1, replica_groups=mesh['dom'=32,'head'=8] {'head'}, use_global_device_ids=true, to_apply=%region_8.9 | all-reduce | flops 2048 | bytes 16384 | tf_op jit(solution)/shard_map/psum | solution.py:114
  277.1 0.7 subtract_multiply_fusion
  277.9 0.3 reduce-scatter.2.cloned.1.call-start
  278.1 26.5 %all-gather.5.cloned.1.call-done = f32[1024,512]{0,1:T(8,128)} async-done(((f32[1024,64]{0,1:T(8,128)}), f32[1024,512]{0,1:T(8,128)}) %all-gather.5.cloned.1.call-update) | async-done | bytes 2097168 | tf_op jit(solution)/shard_map/all_gather | solution.py:120
  304.6 5.0 %fusion.156 = f32[1024,128]{1,0:T(8,128)S(1)} fusion(f32[1024,512]{0,1:T(8,128)} %all-gather.5.cloned.1.call-done, f32[512,128]{1,0:T(8,128)S(1)} %copy-done.7), kind=kOutput, calls=%fused_computation.221 | convolution fusion | flops 805306368 | bytes 2883584 | tf_op jit(solution)/shard_map/dot_general | solution.py:28
  309.6 4.3 %fusion.21 = f32[1024,512]{0,1:T(8,128)} fusion(f32[128,512]{1,0:T(8,128)S(1)} %copy-done.10, f32[1024,128]{1,0:T(8,128)S(1)} %fusion.156), kind=kOutput, calls=%fused_computation.37 | convolution fusion | flops 813694976 | bytes 2883584 | tf_op jit(solution)/shard_map/dot_general | solution.py:28
  314.0 36.6 %reduce-scatter.2.cloned.1.call-done = f32[1024,64]{0,1:T(8,128)} async-done(((f32[1024,512]{0,1:T(8,128)}), f32[1024,64]{0,1:T(8,128)}) %reduce-scatter.2.cloned.1.call-update) | async-done | bytes 262160 | tf_op jit(solution)/shard_map/reduce_scatter | solution.py:123
  350.6 1.0 add.130
  351.6 0.2 copy.69
  351.8 3.2 scatter_custom_fusion.1
  355.0 0.9 copy.70
  (62 shorter events, 1.1 us)
Async XLA Ops:
  6.5 17.9 %copy-start = (f32[1024,512]{1,0:T(8,128)S(1)}, f32[1024,512]{1,0:T(8,128)}, u32[]{:S(2)}) copy-start(f32[1024,512]{1,0:T(8,128)} %param.13) | copy-start | bytes 6291460
  12.1 27.0 %all-to-all-start = ((s32[32,1,3]{2,1,0:T(1,128)}), s32[32,1,3]{2,1,0:T(1,128)S(1)}, u32[]{:S(2)}, u32[]{:S(2)}) async-start(s32[32,1,3]{2,1,0:T(1,128)} %copy.52), calls=%async_computation | async-start | bytes 32768 | tf_op jit(solution)/shard_map/all_to_all | solution.py:99
  32.2 1.8 copy-start.5
  32.2 3.3 copy-start.6
  34.0 2.9 copy-start.2
  49.1 148.0 %all-to-all-start.1 = ((f32[32,3,128,128]{3,2,1,0:T(8,128)}), f32[32,3,128,128]{3,2,1,0:T(8,128)}, u32[]{:S(2)}, u32[]{:S(2)}) async-start(f32[32,3,128,128]{3,2,1,0:T(8,128)} %broadcast_select_fusion), calls=%async_computation.1 | async-start | bytes 12582912 | tf_op jit(solution)/shard_map/all_to_all | solution.py:101
  58.9 15.1 %copy-start.9 = (s32[8,6]{1,0:T(8,128)S(1)}, s32[8,6]{1,0:T(8,128)}, u32[]{:S(2)}) copy-start(s32[8,6]{1,0:T(8,128)} %param.17) | copy-start | bytes 580
  58.9 15.2 %copy-start.1 = (s32[256]{0:T(256)S(1)}, s32[256]{0:T(256)}, u32[]{:S(2)}) copy-start(s32[256]{0:T(256)} %param.15) | copy-start | bytes 3076
  58.9 200.9 %all-gather.3.cloned.1.call-start = ((), (), s32[]{:S(2)}) async-start(), calls=%async_computation.3 | async-start | bytes 2359296 | tf_op jit(solution)/shard_map/all_gather | solution.py:111
  61.3 23.9 %collective-permute-start.1 = (f32[2,128,128]{2,1,0:T(8,128)}, f32[2,128,128]{2,1,0:T(8,128)}, u32[]{:S(2)}, u32[]{:S(2)}) collective-permute-start(f32[2,128,128]{2,1,0:T(8,128)} %bitcast.1), channel_id=1, source_target_pairs={{8,0},{16,8},{24,16},{32,24},{40,32},{48,40},{56,48},{64,56},{72,6... | collective-permute-start | bytes 393224 | tf_op jit(solution)/shard_map/ppermute | solution.py:22
  64.3 20.9 %collective-permute-start = (f32[2,128,128]{2,1,0:T(8,128)}, f32[2,128,128]{2,1,0:T(8,128)}, u32[]{:S(2)}, u32[]{:S(2)}) collective-permute-start(f32[2,128,128]{2,1,0:T(8,128)} %bitcast), channel_id=1, source_target_pairs={{0,8},{8,16},{16,24},{24,32},{32,40},{40,48},{48,56},{56,64},{64,7... | collective-permute-start | bytes 393224 | tf_op jit(solution)/shard_map/ppermute | solution.py:21
  74.9 1.2 copy-start.11
  197.0 5.4 %copy-start.3 = (f32[8,1,128,128]{3,2,1,0:T(8,128)S(1)}, f32[8,1,128,128]{3,2,1,0:T(8,128)}, u32[]{:S(2)}) copy-start(f32[8,1,128,128]{3,2,1,0:T(8,128)} %fusion.23) | copy-start | bytes 1572868
  202.5 2.8 copy-start.4
  212.5 47.3 %copy-start.8 = (f32[512,64]{0,1:T(8,128)S(1)}, f32[512,64]{0,1:T(8,128)}, u32[]{:S(2)}) copy-start(f32[512,64]{0,1:T(8,128)} %param.23) | copy-start | bytes 393220
  223.0 81.6 %copy-start.7 = (f32[512,128]{1,0:T(8,128)S(1)}, f32[512,128]{1,0:T(8,128)}, u32[]{:S(2)}) copy-start(f32[512,128]{1,0:T(8,128)} %param.24) | copy-start | bytes 786436
  224.0 80.6 %all-gather.5.cloned.1.call-start = ((), (), s32[]{:S(2)}) async-start(), calls=%async_computation.4 | async-start | bytes 2359296 | tf_op jit(solution)/shard_map/all_gather | solution.py:120
  224.0 85.6 %copy-start.10 = (f32[128,512]{1,0:T(8,128)S(1)}, f32[128,512]{1,0:T(8,128)}, u32[]{:S(2)}) copy-start(f32[128,512]{1,0:T(8,128)} %param.25) | copy-start | bytes 786436
  277.9 72.7 %reduce-scatter.2.cloned.1.call-start = ((), (), s32[]{:S(2)}) async-start(), calls=%async_computation.5 | async-start | bytes 2359296 | tf_op jit(solution)/shard_map/reduce_scatter | solution.py:123
Sparse Core Ops, SparseCore 0:
  224.1 35.6 all-gather.2
  278.0 26.5 all-gather.4
  314.1 36.4 reduce-scatter.1
where the time goes:
time: 368 us; the launch traced here: 363 us
  waiting for transfers between devices  209 us (57%)
  matrix products  40.4 us (11%)
  local copies, waits for them, and re-layouts  36.7 us (10%)
  starting transfers between devices  28.1 us (8%)
  other arithmetic  20.9 us (6%)
  blocking collectives  14.2 us (4%)
  between operations  13.7 us (4%)
    all_to_all x1, waiting for transfers between devices, shards(): lax.all_to_all(blocks, 'dom', split_axis=0, concat_axis=0, tiled=True)  106 us
    reduce_scatter x1, waiting for transfers between devices, shards(): lax.psum_scatter(partials, 'head', scatter_dimension=1, tiled=True)  36.6 us
    all_gather x1, waiting for transfers between devices, shards(): lax.all_gather(heads_flat, 'head', axis=1, tiled=True)  35.8 us
    all_gather x1, waiting for transfers between devices, shards(): hidden = matmul(lax.all_gather(normed, 'head', axis=1, tiled=True), w_up)  26.5 us
    dot_general x8, matrix products, matmul(): jnp.dot(left, right, preferred_element_type=jnp.float32, precision=highest)  23.7 us
    psum x1, blocking collectives, shards(): lax.psum((jnp.sum(residual, 1), jnp.sum(residual * residual, 1)), 'head')  14.2 us
    all_to_all x1, starting transfers between devices, shards(): lax.all_to_all(request, 'dom', split_axis=0, concat_axis=0, tiled=True)  11.6 us
    dot_general x1, matrix products, partial_softmax(): jnp.einsum('bhqk,bkhd->bqhd', weights, value_rows, precision=highest)  10.5 us
  transfers between devices with their start and end apart: 7, of which 5 were waited for; matrix products, arithmetic and copies ran while one was open for 10% of the time, Pallas kernels for 0%

commit v1 on v0

--- a/solution.py
+++ b/solution.py
@@ -9,6 +9,13 @@
 NE = 6
 LW = 2
 highest = lax.Precision.HIGHEST
+
+
+def limits_fix(local_values, at_axis):
+    part_now = list(local_values.shape[1:])
+    part_now[at_axis] *= local_values.shape[0]
+    block_last = jnp.moveaxis(local_values, 0, at_axis).reshape(part_now)
+    return block_last
 
 
 def with_halo(value, sides, width):
@@ -117,7 +124,31 @@
     row_mean = row_sums / D
     row_var = row_squares / D - row_mean * row_mean
     normed = (residual - row_mean[:, None]) * lax.rsqrt(row_var + 1e-05)[:, None]
-    hidden = matmul(lax.all_gather(normed, "head", axis=1, tiled=True), w_up)
+
+    def recast_cube_here(v0, dev_axis, array_dim):
+        axis_len = lax.axis_size(dev_axis)
+        buffers = []
+        for idx in [*range(axis_len)]:
+            buffers.append((idx, (idx + 1) % axis_len))
+        rack = []
+        for p, dev in buffers:
+            rack.append((dev, p))
+        a_now, then = ([], [])
+        for ix in [*range(axis_len - 1)]:
+            if ix % 2 == 0:
+                placed = lax.ppermute(a_now[-1] if a_now else v0, axis_name=dev_axis, perm=buffers)
+                a_now.append(placed)
+            else:
+                then.append(lax.ppermute(then[-1] if then else v0, axis_name=dev_axis, perm=rack))
+        mixed_arr = jnp.stack([*a_now[::-1], v0, *then], axis=0)
+        out_arr = lax.axis_index(dev_axis)
+        local_part = len(a_now)
+        carry = out_arr - local_part
+        mixed_arr = mixed_arr[(jnp.arange(axis_len) - carry) % axis_len]
+        state_next = limits_fix(mixed_arr, array_dim)
+        return state_next
+
+    hidden = matmul(recast_cube_here(normed, "head", 1), w_up)
     activated = jax.nn.gelu(hidden, approximate=False)
     partials = matmul(activated, w_down)
     feed_forward = lax.psum_scatter(partials, "head", scatter_dimension=1, tiled=True)

time: 368 us -> 381 us (1.035)
  local copies, waits for them, and re-layouts: 36.7 us -> 47.4 us
  waiting for transfers between devices: 209 us -> 200 us
  starting transfers between devices: 28.1 us -> 36.7 us
    all_gather x1 -> x0, waiting for transfers between devices: 26.5 us -> none  [shards(): hidden = matmul(lax.all_gather(normed, 'head', axis=1, tiled=True), w_up)]
    ppermute x0 -> x7, waiting for transfers between devices: none -> 19.5 us  [the longest x4 19.5 us: recast_cube_here(): lax.ppermute(a_now[-1] if a_now else v0, axis_name=dev_axis, perm=buffers)]
    ppermute x0 -> x7, starting transfers between devices: none -> 8.9 us  [the longest x3 8.87 us: recast_cube_here(): lax.ppermute(then[-1] if then else v0, axis_name=dev_axis, perm=rack)]
    unnamed x26 -> x34, local copies, waits for them, and re-layouts: 1.57 us -> 7.82 us
  transfers between devices with their start and end apart: 7 -> 13, of which waited for: 5 -> 8; matrix products, arithmetic and copies ran while one was open for 10% -> 12% of each run, Pallas kernels for 0% -> 0%
where the time goes in v1:
time: 381 us; the launch traced here: 375 us
  waiting for transfers between devices  200 us (52%)
  local copies, waits for them, and re-layouts  47.4 us (12%)
  matrix products  40.4 us (11%)
  starting transfers between devices  36.7 us (10%)
  other arithmetic  21.6 us (6%)
  blocking collectives  14.5 us (4%)
  between operations  14 us (4%)
    all_to_all x1, waiting for transfers between devices, shards(): lax.all_to_all(blocks, 'dom', split_axis=0, concat_axis=0, tiled=True)  106 us
    all_gather x1, waiting for transfers between devices, shards(): lax.all_gather(heads_flat, 'head', axis=1, tiled=True)  35.8 us
    reduce_scatter x1, waiting for transfers between devices, shards(): lax.psum_scatter(partials, 'head', scatter_dimension=1, tiled=True)  35.2 us
    dot_general x8, matrix products, matmul(): jnp.dot(left, right, preferred_element_type=jnp.float32, precision=highest)  23.8 us
    ppermute x4, waiting for transfers between devices, recast_cube_here(): lax.ppermute(a_now[-1] if a_now else v0, axis_name=dev_axis, perm=buffers)  19.5 us
    psum x1, blocking collectives, shards(): lax.psum((jnp.sum(residual, 1), jnp.sum(residual * residual, 1)), 'head')  14.5 us
    all_to_all x1, starting transfers between devices, shards(): lax.all_to_all(request, 'dom', split_axis=0, concat_axis=0, tiled=True)  11.6 us
    dot_general x1, matrix products, partial_softmax(): jnp.einsum('bhqk,bkhd->bqhd', weights, value_rows, precision=highest)  10.5 us
  transfers between devices with their start and end apart: 13, of which 8 were waited for; matrix products, arithmetic and copies ran while one was open for 12% of the time, Pallas kernels for 0%

profile of v1, /device:TPU:2, one launch (start us, length us, event | category | flops | bytes accessed | tf_op | source)
XLA Modules:
  0.0 374.9 jit_solution(15892633168308145555)
XLA Ops:
  6.5 0.9 reshape.284
  7.5 0.8 reshape.283
  8.6 2.8 scatter_fusion
  11.4 0.7 copy.52
  12.1 11.6 %all-to-all-start = ((s32[32,1,3]{2,1,0:T(1,128)}), s32[32,1,3]{2,1,0:T(1,128)S(1)}, u32[]{:S(2)}, u32[]{:S(2)}) async-start(s32[32,1,3]{2,1,0:T(1,128)} %copy.52), calls=%async_computation | async-start | bytes 32768 | tf_op jit(solution)/shard_map/all_to_all | solution.py:106
  24.4 0.7 compare_and_fusion.1
  25.1 4.9 %gather_fusion = f32[1024,512]{1,0:T(8,128)} fusion(f32[1024,512]{1,0:T(8,128)S(1)} %copy-done, s32[1024]{0:T(1024)S(1)} %broadcast_clamp_fusion), kind=kCustom, calls=%fused_computation | custom fusion | bytes 4198400 | tf_op jit(solution)/shard_map/jit(_take)/gather | solution.py:80
  30.0 2.9 copy.47
  32.9 1.8 broadcast_select_fusion.1
  34.7 1.5 fusion.155
  36.2 1.5 fusion.154
  37.7 0.8 pad_maximum_fusion.2
  38.5 1.2 copy.74
  40.2 3.6 gather_fusion.2
  43.9 5.9 %broadcast_select_fusion = f32[32,3,128,128]{3,2,1,0:T(8,128)} fusion(f32[32,3,128,128]{3,2,1,0:T(8,128)} %bitcast.103, pred[32,3]{1,0:T(8,128)(4,1)S(1)} %copy.54), kind=kLoop, calls=%fused_computation.18 | loop fusion | flops 1572864 | bytes 12583008 | tf_op jit(solution)/shard_map/jit(_take)/select_n | solution.py:105
  49.8 9.8 %all-to-all-start.1 = ((f32[32,3,128,128]{3,2,1,0:T(8,128)}), f32[32,3,128,128]{3,2,1,0:T(8,128)}, u32[]{:S(2)}, u32[]{:S(2)}) async-start(f32[32,3,128,128]{3,2,1,0:T(8,128)} %broadcast_select_fusion), calls=%async_computation.1 | async-start | bytes 12582912 | tf_op jit(solution)/shard_map/all_to_all | solution.py:108
  59.6 0.7 fusion.113
  60.3 1.7 copy.72
  62.0 2.2 collective-permute-start.1
  64.2 0.8 copy.71
  65.0 4.1 %collective-permute-start = (f32[2,128,128]{2,1,0:T(8,128)}, f32[2,128,128]{2,1,0:T(8,128)}, u32[]{:S(2)}, u32[]{:S(2)}) collective-permute-start(f32[2,128,128]{2,1,0:T(8,128)} %bitcast), channel_id=1, source_target_pairs={{0,8},{8,16},{16,24},{24,32},{32,40},{40,48},{48,56},{56,64},{64,7... | collective-permute-start | bytes 393224 | tf_op jit(solution)/shard_map/ppermute | solution.py:28
  69.1 2.4 fusion.157
  71.4 2.4 fusion.156
  73.9 0.8 copy.48
  75.0 0.8 gather_fusion.6
  76.0 0.7 gather_fusion.5
  76.9 3.7 convolution_bitcast_fusion
  81.5 0.9 fusion.23
  82.4 3.4 collective-permute-done.1
  85.9 1.0 pad_maximum_fusion.1
  86.9 1.8 gather_fusion.1
  88.7 2.7 broadcast_select_fusion.2
  91.4 106.3 %all-to-all-done.1 = f32[32,3,128,128]{3,2,1,0:T(8,128)} async-done(((f32[32,3,128,128]{3,2,1,0:T(8,128)}), f32[32,3,128,128]{3,2,1,0:T(8,128)}, u32[]{:S(2)}, u32[]{:S(2)}) %all-to-all-start.1) | async-done | bytes 6291488 | tf_op jit(solution)/shard_map/all_to_all | solution.py:108
  197.7 5.4 %gather_fusion.3 = f32[48,128,128]{2,1,0:T(8,128)} fusion(f32[32,3,128,128]{3,2,1,0:T(8,128)} %all-to-all-done.1, s32[48]{0:T(128)S(1)} %get-tuple-element.11), kind=kCustom, calls=%fused_computation.3 | custom fusion | bytes 6291840 | tf_op jit(solution)/shard_map/gather | solution.py:109
  203.1 2.8 pad_maximum_fusion
  205.9 6.1 %fusion.153 = (f32[8,128]{1,0:T(8,128)S(1)}, f32[8,128,1280]{2,1,0:T(8,128)S(1)}) fusion(f32[8,1280,128]{2,1,0:T(8,128)S(1)} %bitcast.101, f32[8,8,8,128]{3,2,1,0:T(8,128)S(1)} %copy-done.4, pred[8,1280]{1,0:T(8,128)(4,1)S(1)} %add_bitcast_fusion), kind=kOutput, calls=%fused_computation.232 | convolution fusion | flops 1010564096 | bytes 10762240 | tf_op jit(solution)/shard_map/bqhd,bkhd->bhqk/dot_general | solution.py:44
  212.0 1.1 fusion.6
  213.2 10.5 %fusion.16 = f32[8,128,1,64]{1,3,0,2:T(8,128)S(1)} fusion(f32[8,128,1280]{2,1,0:T(8,128)S(1)} %get-tuple-element.22, f32[8,128]{1,0:T(8,128)S(1)} %get-tuple-element.21, pred[8,1280]{1,0:T(8,128)(4,1)S(1)} %add_bitcast_fusion, f32[8,1280,128]{2,1,0:T(8,128)S(1)} %bitcast.102, f32[8,128]{1,0:T(8,128)S(1)} %fusion.6), kind=kOutput, calls=%fused_computation.26 | convolution fusion | flops 1009319936 | bytes 10766336 | tf_op jit(solution)/shard_map/bhqk,bkhd->bqhd/dot_general | solution.py:51
  223.9 0.8 copy.86
  224.7 35.8 %all-gather.2.cloned.1.call-done = f32[1024,512]{0,1:T(8,128)} async-done(((f32[1024,64]{0,1:T(8,128)}), f32[1024,512]{0,1:T(8,128)}) %all-gather.2.cloned.1.call-update) | async-done | bytes 2097168 | tf_op jit(solution)/shard_map/all_gather | solution.py:118
  260.5 3.0 fusion.152
  263.5 14.5 %all-reduce = (f32[1024]{0:T(1024)S(1)}, f32[1024]{0:T(1024)S(1)}) all-reduce(f32[1024]{0:T(1024)S(1)} %get-tuple-element.6, f32[1024]{0:T(1024)S(1)} %get-tuple-element.5), channel_id=1, replica_groups=mesh['dom'=32,'head'=8] {'head'}, use_global_device_ids=true, to_apply=%region_8.9 | all-reduce | flops 2048 | bytes 16384 | tf_op jit(solution)/shard_map/psum | solution.py:121
  278.1 7.0 %collective-permute-done.2 = f32[1024,64]{0,1:T(8,128)S(1)} collective-permute-done((f32[1024,64]{0,1:T(8,128)S(1)}, f32[1024,64]{0,1:T(8,128)S(1)}, u32[]{:S(2)}, u32[]{:S(2)}) %collective-permute-start.2) | collective-permute-done | bytes 262176 | tf_op jit(solution)/shard_map/ppermute | solution.py:139
  285.1 3.0 collective-permute-start.6
  288.0 4.1 %collective-permute-done.3 = f32[1024,64]{0,1:T(8,128)S(1)} collective-permute-done((f32[1024,64]{0,1:T(8,128)S(1)}, f32[1024,64]{0,1:T(8,128)S(1)}, u32[]{:S(2)}, u32[]{:S(2)}) %collective-permute-start.3) | collective-permute-done | bytes 262176 | tf_op jit(solution)/shard_map/ppermute | solution.py:139
  292.1 3.0 collective-permute-start.7
  295.0 4.2 %collective-permute-done.4 = f32[1024,64]{0,1:T(8,128)} collective-permute-done((f32[1024,64]{0,1:T(8,128)S(1)}, f32[1024,64]{0,1:T(8,128)}, u32[]{:S(2)}, u32[]{:S(2)}) %collective-permute-start.4) | collective-permute-done | bytes 262176 | tf_op jit(solution)/shard_map/ppermute | solution.py:139
  299.2 3.0 collective-permute-start.8
  302.2 4.3 %collective-permute-done.5 = f32[1024,64]{0,1:T(8,128)} collective-permute-done((f32[1024,64]{0,1:T(8,128)}, f32[1024,64]{0,1:T(8,128)}, u32[]{:S(2)}, u32[]{:S(2)}) %collective-permute-start.5) | collective-permute-done | bytes 262176 | tf_op jit(solution)/shard_map/ppermute | solution.py:139
  306.5 1.7 bitcast_dynamic-update-slice_fusion.7
  308.2 1.7 bitcast_dynamic-update-slice_fusion.6
  309.9 0.7 bitcast_dynamic-update-slice_fusion.5
  310.6 0.7 bitcast_dynamic-update-slice_fusion.4
  311.3 0.7 bitcast_dynamic-update-slice_fusion.3
  312.1 0.7 bitcast_dynamic-update-slice_fusion.2
  312.8 0.7 bitcast_dynamic-update-slice_fusion.1
  313.5 0.7 bitcast_dynamic-update-slice_fusion
  314.3 3.6 gather_fusion.7
  317.9 5.1 %fusion.158 = f32[1024,128]{1,0:T(8,128)S(1)} fusion(f32[1024,512]{0,1:T(8,128)} %bitcast.104, f32[512,128]{1,0:T(8,128)S(1)} %copy-done.7), kind=kOutput, calls=%fused_computation.237 | convolution fusion | flops 805306368 | bytes 2883584 | tf_op jit(solution)/shard_map/dot_general | solution.py:35
  323.0 4.3 %fusion.21 = f32[1024,512]{0,1:T(8,128)} fusion(f32[128,512]{1,0:T(8,128)S(1)} %copy-done.11, f32[1024,128]{1,0:T(8,128)S(1)} %fusion.158), kind=kOutput, calls=%fused_computation.38 | convolution fusion | flops 813694976 | bytes 2883584 | tf_op jit(solution)/shard_map/dot_general | solution.py:35
  327.3 35.2 %reduce-scatter.2.cloned.1.call-done = f32[1024,64]{0,1:T(8,128)} async-done(((f32[1024,512]{0,1:T(8,128)}), f32[1024,64]{0,1:T(8,128)}) %reduce-scatter.2.cloned.1.call-update) | async-done | bytes 262160 | tf_op jit(solution)/shard_map/reduce_scatter | solution.py:154
  362.5 1.0 add.156
  363.7 3.2 scatter_custom_fusion.1
  366.9 0.9 copy.70
  (84 shorter events, 3.8 us)
Async XLA Ops:
  6.5 18.5 %copy-start = (f32[1024,512]{1,0:T(8,128)S(1)}, f32[1024,512]{1,0:T(8,128)}, u32[]{:S(2)}) copy-start(f32[1024,512]{1,0:T(8,128)} %param.13) | copy-start | bytes 6291460
  12.1 27.7 %all-to-all-start = ((s32[32,1,3]{2,1,0:T(1,128)}), s32[32,1,3]{2,1,0:T(1,128)S(1)}, u32[]{:S(2)}, u32[]{:S(2)}) async-start(s32[32,1,3]{2,1,0:T(1,128)} %copy.52), calls=%async_computation | async-start | bytes 32768 | tf_op jit(solution)/shard_map/all_to_all | solution.py:106
  32.9 1.8 copy-start.5
  34.7 2.9 copy-start.2
  34.7 1.5 copy-start.6
  49.8 148.0 %all-to-all-start.1 = ((f32[32,3,128,128]{3,2,1,0:T(8,128)}), f32[32,3,128,128]{3,2,1,0:T(8,128)}, u32[]{:S(2)}, u32[]{:S(2)}) async-start(f32[32,3,128,128]{3,2,1,0:T(8,128)} %broadcast_select_fusion), calls=%async_computation.1 | async-start | bytes 12582912 | tf_op jit(solution)/shard_map/all_to_all | solution.py:108
  59.6 200.9 %all-gather.2.cloned.1.call-start = ((), (), s32[]{:S(2)}) async-start(), calls=%async_computation.3 | async-start | bytes 2359296 | tf_op jit(solution)/shard_map/all_gather | solution.py:118
  60.3 14.5 %copy-start.10 = (s32[8,6]{1,0:T(8,128)S(1)}, s32[8,6]{1,0:T(8,128)}, u32[]{:S(2)}) copy-start(s32[8,6]{1,0:T(8,128)} %param.17) | copy-start | bytes 580
  60.3 14.7 %copy-start.1 = (s32[256]{0:T(256)S(1)}, s32[256]{0:T(256)}, u32[]{:S(2)}) copy-start(s32[256]{0:T(256)} %param.15) | copy-start | bytes 3076
  62.0 23.8 %collective-permute-start.1 = (f32[2,128,128]{2,1,0:T(8,128)}, f32[2,128,128]{2,1,0:T(8,128)}, u32[]{:S(2)}, u32[]{:S(2)}) collective-permute-start(f32[2,128,128]{2,1,0:T(8,128)} %bitcast.1), channel_id=1, source_target_pairs={{8,0},{16,8},{24,16},{32,24},{40,32},{48,40},{56,48},{64,56},{72,6... | collective-permute-start | bytes 393224 | tf_op jit(solution)/shard_map/ppermute | solution.py:29
  65.0 20.9 %collective-permute-start = (f32[2,128,128]{2,1,0:T(8,128)}, f32[2,128,128]{2,1,0:T(8,128)}, u32[]{:S(2)}, u32[]{:S(2)}) collective-permute-start(f32[2,128,128]{2,1,0:T(8,128)} %bitcast), channel_id=1, source_target_pairs={{0,8},{8,16},{16,24},{24,32},{32,40},{40,48},{48,56},{56,64},{64,7... | collective-permute-start | bytes 393224 | tf_op jit(solution)/shard_map/ppermute | solution.py:28
  76.0 1.0 copy-start.8
  76.7 4.0 %copy-start.12 = (s32[8]{0:T(128)S(1)}, s32[8]{0:T(128)}, u32[]{:S(2)}) copy-start(s32[8]{0:T(128)} %param.18) | copy-start | bytes 100
  197.7 5.4 %copy-start.3 = (f32[8,1,128,128]{3,2,1,0:T(8,128)S(1)}, f32[8,1,128,128]{3,2,1,0:T(8,128)}, u32[]{:S(2)}) copy-start(f32[8,1,128,128]{3,2,1,0:T(8,128)} %fusion.23) | copy-start | bytes 1572868
  203.1 2.8 copy-start.4
  213.2 47.3 %copy-start.9 = (f32[512,64]{0,1:T(8,128)S(1)}, f32[512,64]{0,1:T(8,128)}, u32[]{:S(2)}) copy-start(f32[512,64]{0,1:T(8,128)} %param.23) | copy-start | bytes 393220
  224.7 137.9 %reduce-scatter.2.cloned.1.call-start = ((), (), s32[]{:S(2)}) async-start(), calls=%async_computation.4 | async-start | bytes 2359296 | tf_op jit(solution)/shard_map/reduce_scatter | solution.py:154
  278.0 7.0 %collective-permute-start.2 = (f32[1024,64]{0,1:T(8,128)S(1)}, f32[1024,64]{0,1:T(8,128)S(1)}, u32[]{:S(2)}, u32[]{:S(2)}) collective-permute-start(f32[1024,64]{0,1:T(8,128)S(1)} %subtract_multiply_fusion), channel_id=1, source_target_pairs={{0,1},{1,2},{2,3},{3,4},{4,5},{5,6},{6,7},{7,0},{8,9},{9,10},{10,1... | collective-permute-start | bytes 786440 | tf_op jit(solution)/shard_map/ppermute | solution.py:139
  285.1 7.0 %collective-permute-start.3 = (f32[1024,64]{0,1:T(8,128)S(1)}, f32[1024,64]{0,1:T(8,128)S(1)}, u32[]{:S(2)}, u32[]{:S(2)}) collective-permute-start(f32[1024,64]{0,1:T(8,128)S(1)} %collective-permute-done.2), channel_id=1, source_target_pairs={{0,1},{1,2},{2,3},{3,4},{4,5},{5,6},{6,7},{7,0},{8,9},{9,10},{10,1... | collective-permute-start | bytes 786440 | tf_op jit(solution)/shard_map/ppermute | solution.py:139
  285.1 7.0 %collective-permute-start.6 = (f32[1024,64]{0,1:T(8,128)S(1)}, f32[1024,64]{0,1:T(8,128)S(1)}, u32[]{:S(2)}, u32[]{:S(2)}) collective-permute-start(f32[1024,64]{0,1:T(8,128)S(1)} %subtract_multiply_fusion), channel_id=1, source_target_pairs={{1,0},{2,1},{3,2},{4,3},{5,4},{6,5},{7,6},{0,7},{9,8},{10,9},{11,1... | collective-permute-start | bytes 786440 | tf_op jit(solution)/shard_map/ppermute | solution.py:142
  292.1 7.1 %collective-permute-start.4 = (f32[1024,64]{0,1:T(8,128)S(1)}, f32[1024,64]{0,1:T(8,128)}, u32[]{:S(2)}, u32[]{:S(2)}) collective-permute-start(f32[1024,64]{0,1:T(8,128)S(1)} %collective-permute-done.3), channel_id=1, source_target_pairs={{0,1},{1,2},{2,3},{3,4},{4,5},{5,6},{6,7},{7,0},{8,9},{9,10},{10,1... | collective-permute-start | bytes 786440 | tf_op jit(solution)/shard_map/ppermute | solution.py:139
  292.1 7.1 %collective-permute-start.7 = (f32[1024,64]{0,1:T(8,128)S(1)}, f32[1024,64]{0,1:T(8,128)S(1)}, u32[]{:S(2)}, u32[]{:S(2)}) collective-permute-start(f32[1024,64]{0,1:T(8,128)S(1)} %collective-permute-done.6), channel_id=1, source_target_pairs={{1,0},{2,1},{3,2},{4,3},{5,4},{6,5},{7,6},{0,7},{9,8},{10,9},{11,1... | collective-permute-start | bytes 786440 | tf_op jit(solution)/shard_map/ppermute | solution.py:142
  299.2 7.3 %collective-permute-start.5 = (f32[1024,64]{0,1:T(8,128)}, f32[1024,64]{0,1:T(8,128)}, u32[]{:S(2)}, u32[]{:S(2)}) collective-permute-start(f32[1024,64]{0,1:T(8,128)} %collective-permute-done.4), channel_id=1, source_target_pairs={{0,1},{1,2},{2,3},{3,4},{4,5},{5,6},{6,7},{7,0},{8,9},{9,10},{10,1... | collective-permute-start | bytes 786440 | tf_op jit(solution)/shard_map/ppermute | solution.py:139
  299.2 14.3 %collective-permute-start.8 = (f32[1024,64]{0,1:T(8,128)S(1)}, f32[1024,64]{0,1:T(8,128)S(1)}, u32[]{:S(2)}, u32[]{:S(2)}) collective-permute-start(f32[1024,64]{0,1:T(8,128)S(1)} %collective-permute-done.7), channel_id=1, source_target_pairs={{1,0},{2,1},{3,2},{4,3},{5,4},{6,5},{7,6},{0,7},{9,8},{10,9},{11,1... | collective-permute-start | bytes 786440 | tf_op jit(solution)/shard_map/ppermute | solution.py:142
  314.3 3.6 copy-start.7
  317.9 5.1 %copy-start.11 = (f32[128,512]{1,0:T(8,128)S(1)}, f32[128,512]{1,0:T(8,128)}, u32[]{:S(2)}) copy-start(f32[128,512]{1,0:T(8,128)} %param.25) | copy-start | bytes 786436
Sparse Core Ops, SparseCore 0:
  224.8 35.6 all-gather.1
  327.4 35.0 reduce-scatter.1
